TPU v7x, 32 devices: a whole 2x2x4 slice. The times are simulated.
32 devices in a mesh: section: 4 (over y, x), rep: 8 (over z, core).
Axes of the slice: x: 2, y: 2, z: 4, core: 2. Of those that a mesh axis runs over, the one named last changes fastest.
Arguments:
- x_in: bfloat16 [1024, 4096], P('rep'), may hold values from -6 to 6
- cot: bfloat16 [1024, 4096], P('rep'), may hold values from -6 to 6
- w_q: bfloat16 [4, 4096, 128], P('section', 'rep'), may hold values from -0.09375 to 0.09375
- w_k: bfloat16 [4, 4096, 128], P('section', 'rep'), may hold values from -0.09375 to 0.09375
- w_v: bfloat16 [4, 4096, 128], P('section', 'rep'), may hold values from -0.09375 to 0.09375
- w_out: bfloat16 [4, 4096, 128], P('section', 'rep'), may hold values from -0.5 to 0.5
- gains: float32 [4, 4096], P('section'), may hold values from 0.5 to 1.5
- offsets: int32 [4, 8], replicated, may hold values from 0 to 7
- counts: int32 [4, 8], replicated, may hold values from 1 to 8
Outputs:
- grad_q: float32 [4, 4096, 128], P('section', 'rep')
- grad_k: float32 [4, 4096, 128], P('section', 'rep')
- grad_v: float32 [4, 4096, 128], P('section', 'rep')
- grad_o: float32 [4, 4096, 128], P('section', 'rep')
All inputs are finite; a program needn't handle non-finite values.
Results may differ from a plain program's by a relative error of at most 0.023.
Values may be sent and summed in bfloat16 or wider, within the bound.
A program may use at most 64 MiB of HBM per device.

v0:
```python
import jax
import jax.numpy as jnp
from jax import lax
from jax.sharding import PartitionSpec as P

MB = 8
ROWS = 16
EPSILON = 1e-05


def from_behind(block, axis, distance):
    devices = range(lax.axis_size(axis))
    route = [(i - distance, i) for i in devices if i - distance in devices]
    return lax.ppermute(block, axis, route)


def attend(query, key, scale):
    rows_here = query.shape[0]
    scores = jnp.einsum("id,jd->ij", query, key, preferred_element_type=jnp.float32) * scale
    causal = jnp.arange(rows_here)[:, None] >= jnp.arange(rows_here)[None, :]
    expo = jnp.exp(jnp.where(causal, scores, -1e30))
    return expo / jnp.sum(expo, axis=-1, keepdims=True)


def forward_layer(layer_in, gain, weights, keep):
    weight_q, weight_k, weight_v, weight_o = weights
    scale = weight_q.shape[1] ** (-0.5)
    x_float = layer_in.astype(jnp.float32)
    rinv = lax.rsqrt(jnp.mean(x_float * x_float, axis=-1, keepdims=True) + EPSILON)
    normed = (x_float * rinv * gain).astype(jnp.bfloat16)
    query = jnp.dot(normed, weight_q, preferred_element_type=jnp.float32).astype(jnp.bfloat16)
    key = jnp.dot(normed, weight_k, preferred_element_type=jnp.float32).astype(jnp.bfloat16)
    value = jnp.dot(normed, weight_v, preferred_element_type=jnp.float32).astype(jnp.bfloat16)
    probs_low = attend(query, key, scale).astype(jnp.bfloat16)
    heads = jnp.dot(probs_low, value, preferred_element_type=jnp.float32).astype(jnp.bfloat16)
    output = lax.dot_general(
        heads, weight_o, (((1,), (1,)), ((), ())), preferred_element_type=jnp.float32
    )
    result = (x_float + keep * output).astype(jnp.bfloat16)
    return (result, normed, query, key, value, heads)


def backward_layer(grad_in, layer_in, query, key, value, gain, weights, keep):
    weight_q, weight_k, weight_v, weight_o = weights
    scale = weight_q.shape[1] ** (-0.5)
    grad_float = grad_in.astype(jnp.float32)
    grad_rows = (keep * grad_float).astype(jnp.bfloat16)
    d_heads = jnp.dot(grad_rows, weight_o, preferred_element_type=jnp.float32).astype(jnp.bfloat16)
    probs = attend(query, key, scale)
    probs_low = probs.astype(jnp.bfloat16)
    d_value = jnp.einsum(
        "ij,id->jd", probs_low, d_heads, preferred_element_type=jnp.float32
    ).astype(jnp.bfloat16)
    d_probs = jnp.einsum("id,jd->ij", d_heads, value, preferred_element_type=jnp.float32)
    d_score = (probs * (d_probs - jnp.sum(probs * d_probs, axis=-1, keepdims=True)) * scale).astype(
        jnp.bfloat16
    )
    d_query = jnp.dot(d_score, key, preferred_element_type=jnp.float32).astype(jnp.bfloat16)
    d_key = jnp.einsum("ij,id->jd", d_score, query, preferred_element_type=jnp.float32).astype(
        jnp.bfloat16
    )
    contract = (((1,), (1,)), ((), ()))
    d_normed = lax.dot_general(d_query, weight_q, contract, preferred_element_type=jnp.float32)
    d_normed = d_normed + lax.dot_general(
        d_key, weight_k, contract, preferred_element_type=jnp.float32
    )
    d_normed = d_normed + lax.dot_general(
        d_value, weight_v, contract, preferred_element_type=jnp.float32
    )
    x_float = layer_in.astype(jnp.float32)
    rinv = lax.rsqrt(jnp.mean(x_float * x_float, axis=-1, keepdims=True) + EPSILON)
    scaled = d_normed * gain
    d_input = rinv * (
        scaled - x_float * rinv * rinv * jnp.mean(scaled * x_float, axis=-1, keepdims=True)
    )
    return ((grad_float + d_input).astype(jnp.bfloat16), grad_rows, d_query, d_key, d_value)


def store_slot(store, value, slot_at, is_valid):
    old_value = lax.dynamic_index_in_dim(store, slot_at, 0, keepdims=False)
    fresh = jnp.where(is_valid, value, old_value)
    return lax.dynamic_update_index_in_dim(store, fresh, slot_at, 0)


def zeros_like_all(values):
    return tuple((jnp.zeros(value.shape, value.dtype) for value in values))


def pick_slot(store, slot_at):
    return lax.dynamic_index_in_dim(store, slot_at, 0, keepdims=False)


def local_grad(left, right):
    width_left = left.shape[-1]
    width_right = right.shape[-1]
    return jnp.einsum(
        "td,th->dh",
        left.reshape(-1, width_left),
        right.reshape(-1, width_right),
        preferred_element_type=jnp.float32,
    )


def on_device(x_in, cot, w_q, w_k, w_v, w_out, gains, offsets, counts):
    section_count = lax.axis_size("section")
    rep_count = lax.axis_size("rep")
    section_pos = lax.axis_index("section")
    rep_pos = lax.axis_index("rep")
    weights = (
        lax.all_gather(w_q[0], "rep", axis=0, tiled=True),
        lax.all_gather(w_k[0], "rep", axis=0, tiled=True),
        lax.all_gather(w_v[0], "rep", axis=0, tiled=True),
        lax.all_gather(w_out[0], "rep", axis=0, tiled=True),
    )
    width = weights[0].shape[0]
    head_size = weights[0].shape[1]
    gain = gains[0]
    landing_sum = jnp.cumsum(offsets, axis=0) % rep_count
    my_offsets = lax.dynamic_index_in_dim(landing_sum, section_pos, 0, keepdims=False)
    landing = (rep_pos + my_offsets) % rep_count
    count_row = lax.dynamic_index_in_dim(counts, section_pos, 0, keepdims=False)
    match_rep = landing[:, None] == jnp.arange(rep_count, dtype=jnp.int32)[None, :]
    allowed = jnp.sum(jnp.where(match_rep, count_row[None, :], 0), axis=1)
    keeps = (jnp.arange(MB, dtype=jnp.int32) < allowed).astype(jnp.float32)
    inputs = x_in.reshape(MB, ROWS, width)
    top_grads = cot.reshape(MB, ROWS, width)
    tick_count = section_count + MB - 1
    row_block = jnp.zeros((ROWS, width), jnp.bfloat16)
    head_block = jnp.zeros((ROWS, head_size), jnp.bfloat16)

    def forward_tick(tick_no, carry):
        inbox, saved_in, saved_normed, saved_q, saved_k, saved_v, saved_heads = carry
        batch_pos = tick_no - section_pos
        is_valid = (batch_pos >= 0) & (batch_pos < MB)
        batch_at = jnp.clip(batch_pos, 0, MB - 1)
        own_rows = pick_slot(inputs, batch_at)
        layer_in = jnp.where(section_pos == 0, own_rows, inbox)
        keep = pick_slot(keeps, batch_at)
        blank = (row_block, row_block, head_block, head_block, head_block, head_block)
        made = lax.cond(
            is_valid,
            lambda rows_in: forward_layer(rows_in, gain, weights, keep),
            lambda rows_in: zeros_like_all(blank),
            layer_in,
        )
        result, normed, query, key, value, heads = made
        saved_in = store_slot(saved_in, layer_in, batch_at, is_valid)
        saved_normed = store_slot(saved_normed, normed, batch_at, is_valid)
        saved_q = store_slot(saved_q, query, batch_at, is_valid)
        saved_k = store_slot(saved_k, key, batch_at, is_valid)
        saved_v = store_slot(saved_v, value, batch_at, is_valid)
        saved_heads = store_slot(saved_heads, heads, batch_at, is_valid)
        inbox = from_behind(result, "section", 1)
        return (inbox, saved_in, saved_normed, saved_q, saved_k, saved_v, saved_heads)

    wide_store = jnp.zeros((MB, ROWS, width), jnp.bfloat16)
    head_store = jnp.zeros((MB, ROWS, head_size), jnp.bfloat16)
    start_fwd = (row_block, wide_store, wide_store, head_store, head_store, head_store, head_store)
    _, saved_in, saved_normed, saved_q, saved_k, saved_v, saved_heads = lax.fori_loop(
        0, tick_count, forward_tick, start_fwd
    )

    def backward_tick(tick_no, carry):
        inbox, saved_rows, saved_dq, saved_dk, saved_dv = carry
        batch_pos = tick_no - (section_count - 1 - section_pos)
        is_valid = (batch_pos >= 0) & (batch_pos < MB)
        batch_at = jnp.clip(batch_pos, 0, MB - 1)
        grad_in = jnp.where(section_pos == section_count - 1, pick_slot(top_grads, batch_at), inbox)
        layer_in = pick_slot(saved_in, batch_at)
        query = pick_slot(saved_q, batch_at)
        key = pick_slot(saved_k, batch_at)
        value = pick_slot(saved_v, batch_at)
        keep = pick_slot(keeps, batch_at)
        blank = (row_block, row_block, head_block, head_block, head_block)
        made = lax.cond(
            is_valid,
            lambda rows_in: backward_layer(
                rows_in, layer_in, query, key, value, gain, weights, keep
            ),
            lambda rows_in: zeros_like_all(blank),
            grad_in,
        )
        grad_back, grad_rows, d_query, d_key, d_value = made
        saved_rows = store_slot(saved_rows, grad_rows, batch_at, is_valid)
        saved_dq = store_slot(saved_dq, d_query, batch_at, is_valid)
        saved_dk = store_slot(saved_dk, d_key, batch_at, is_valid)
        saved_dv = store_slot(saved_dv, d_value, batch_at, is_valid)
        inbox = from_behind(grad_back, "section", -1)
        return (inbox, saved_rows, saved_dq, saved_dk, saved_dv)

    start_bwd = (row_block, wide_store, head_store, head_store, head_store)
    _, saved_rows, saved_dq, saved_dk, saved_dv = lax.fori_loop(
        0, tick_count, backward_tick, start_bwd
    )
    full_q = local_grad(saved_normed, saved_dq)
    full_k = local_grad(saved_normed, saved_dk)
    full_v = local_grad(saved_normed, saved_dv)
    full_o = local_grad(saved_rows, saved_heads)
    share_width = width // rep_count
    totals = (
        lax.psum(full_q.astype(jnp.bfloat16), "rep").astype(jnp.float32),
        lax.psum(full_k.astype(jnp.bfloat16), "rep").astype(jnp.float32),
        lax.psum(full_v.astype(jnp.bfloat16), "rep").astype(jnp.float32),
        lax.psum(full_o.astype(jnp.bfloat16), "rep").astype(jnp.float32),
    )
    parts = tuple(
        (lax.dynamic_slice_in_dim(total, rep_pos * share_width, share_width, 0) for total in totals)
    )
    return (parts[0][None], parts[1][None], parts[2][None], parts[3][None])


def solution(mesh):
    in_specs = (
        P("rep", None),
        P("rep", None),
        P("section", "rep", None),
        P("section", "rep", None),
        P("section", "rep", None),
        P("section", "rep", None),
        P("section", None),
        P(),
        P(),
    )
    out_specs = (
        P("section", "rep", None),
        P("section", "rep", None),
        P("section", "rep", None),
        P("section", "rep", None),
    )
    return jax.shard_map(
        on_device, mesh=mesh, in_specs=in_specs, out_specs=out_specs, check_vma=False
    )
```

profile of v0, /device:TPU:0, one launch (start us, length us, event | category | flops | bytes accessed | tf_op | source)
XLA Modules:
  0.0 682.0 jit_solution(16594448629739413946)
XLA Ops:
  11.5 23.1 %all-gather.9.cloned.1.call-done = bf16[1,4096,128]{2,1,0:T(8,128)(2,1)} async-done(((bf16[1,512,128]{2,1,0:T(8,128)(2,1)}), bf16[1,4096,128]{2,1,0:T(8,128)(2,1)}) %all-gather.9.cloned.1.call-update) | async-done | bytes 1048592 | tf_op jit(solution)/shard_map/all_gather | solution.py:110
  34.6 23.5 %all-gather.11.cloned.1.call-done = bf16[1,4096,128]{2,1,0:T(8,128)(2,1)} async-done(((bf16[1,512,128]{2,1,0:T(8,128)(2,1)}), bf16[1,4096,128]{2,1,0:T(8,128)(2,1)}) %all-gather.11.cloned.1.call-update) | async-done | bytes 1048592 | tf_op jit(solution)/shard_map/all_gather | solution.py:111
  58.1 23.5 %all-gather.13.cloned.1.call-done = bf16[1,4096,128]{2,1,0:T(8,128)(2,1)} async-done(((bf16[1,512,128]{2,1,0:T(8,128)(2,1)}), bf16[1,4096,128]{2,1,0:T(8,128)(2,1)}) %all-gather.13.cloned.1.call-update) | async-done | bytes 1048592 | tf_op jit(solution)/shard_map/all_gather | solution.py:112
  81.6 23.3 %all-gather.15.cloned.1.call-done = bf16[1,4096,128]{2,1,0:T(8,128)(2,1)} async-done(((bf16[1,512,128]{2,1,0:T(8,128)(2,1)}), bf16[1,4096,128]{2,1,0:T(8,128)(2,1)}) %all-gather.15.cloned.1.call-update) | async-done | bytes 1048592 | tf_op jit(solution)/shard_map/all_gather | solution.py:113
  109.6 211.7 %while.49 = (s32[]{:T(128)}, bf16[16,4096]{1,0:T(8,128)(2,1)S(1)}, bf16[8,16,4096]{2,1,0:T(8,128)(2,1)}, bf16[8,16,4096]{2,1,0:T(8,128)(2,1)}, bf16[8,16,128]{2,...) while((s32[]{:T(128)}, bf16[16,4096]{1,0:T(8,128)(2,1)S(1)}, ...), condition=%wide.region_7.8_spmd, body=%wide.region_2.7_spmd.sunk | while | flops 68175368 | bytes 16946660 | solution.py:159
  112.2 8.9 %conditional.4 = (bf16[16,4096]{1,0:T(8,128)(2,1)}, bf16[16,4096]{1,0:T(8,128)(2,1)S(1)}, bf16[16,128]{1,0:T(8,128)(2,1)}, bf16[16,128]{1,0:T(8,128)(2,1)S(1)}, ...) conditional(s32[]{:T(128)} %convert_element_type.174, () %tuple.109, (bf16[16,4096]{1,0:T(8,128)(2,1)S(1)}, ...), branch_computations={%region_3.3_spmd, %region_4.6_spmd} | conditional | flops 67970560 | bytes 14764648 | solution.py:140
  131.8 8.9 %conditional.4 = (bf16[16,4096]{1,0:T(8,128)(2,1)}, bf16[16,4096]{1,0:T(8,128)(2,1)S(1)}, bf16[16,128]{1,0:T(8,128)(2,1)}, bf16[16,128]{1,0:T(8,128)(2,1)S(1)}, ...) conditional(s32[]{:T(128)} %convert_element_type.174, () %tuple.109, (bf16[16,4096]{1,0:T(8,128)(2,1)S(1)}, ...), branch_computations={%region_3.3_spmd, %region_4.6_spmd} | conditional | flops 67970560 | bytes 14764648 | solution.py:140
  151.5 8.9 %conditional.4 = (bf16[16,4096]{1,0:T(8,128)(2,1)}, bf16[16,4096]{1,0:T(8,128)(2,1)S(1)}, bf16[16,128]{1,0:T(8,128)(2,1)}, bf16[16,128]{1,0:T(8,128)(2,1)S(1)}, ...) conditional(s32[]{:T(128)} %convert_element_type.174, () %tuple.109, (bf16[16,4096]{1,0:T(8,128)(2,1)S(1)}, ...), branch_computations={%region_3.3_spmd, %region_4.6_spmd} | conditional | flops 67970560 | bytes 14764648 | solution.py:140
  171.5 8.9 %conditional.4 = (bf16[16,4096]{1,0:T(8,128)(2,1)}, bf16[16,4096]{1,0:T(8,128)(2,1)S(1)}, bf16[16,128]{1,0:T(8,128)(2,1)}, bf16[16,128]{1,0:T(8,128)(2,1)S(1)}, ...) conditional(s32[]{:T(128)} %convert_element_type.174, () %tuple.109, (bf16[16,4096]{1,0:T(8,128)(2,1)S(1)}, ...), branch_computations={%region_3.3_spmd, %region_4.6_spmd} | conditional | flops 67970560 | bytes 14764648 | solution.py:140
  191.8 8.9 %conditional.4 = (bf16[16,4096]{1,0:T(8,128)(2,1)}, bf16[16,4096]{1,0:T(8,128)(2,1)S(1)}, bf16[16,128]{1,0:T(8,128)(2,1)}, bf16[16,128]{1,0:T(8,128)(2,1)S(1)}, ...) conditional(s32[]{:T(128)} %convert_element_type.174, () %tuple.109, (bf16[16,4096]{1,0:T(8,128)(2,1)S(1)}, ...), branch_computations={%region_3.3_spmd, %region_4.6_spmd} | conditional | flops 67970560 | bytes 14764648 | solution.py:140
  212.0 8.9 %conditional.4 = (bf16[16,4096]{1,0:T(8,128)(2,1)}, bf16[16,4096]{1,0:T(8,128)(2,1)S(1)}, bf16[16,128]{1,0:T(8,128)(2,1)}, bf16[16,128]{1,0:T(8,128)(2,1)S(1)}, ...) conditional(s32[]{:T(128)} %convert_element_type.174, () %tuple.109, (bf16[16,4096]{1,0:T(8,128)(2,1)S(1)}, ...), branch_computations={%region_3.3_spmd, %region_4.6_spmd} | conditional | flops 67970560 | bytes 14764648 | solution.py:140
  232.2 8.9 %conditional.4 = (bf16[16,4096]{1,0:T(8,128)(2,1)}, bf16[16,4096]{1,0:T(8,128)(2,1)S(1)}, bf16[16,128]{1,0:T(8,128)(2,1)}, bf16[16,128]{1,0:T(8,128)(2,1)S(1)}, ...) conditional(s32[]{:T(128)} %convert_element_type.174, () %tuple.109, (bf16[16,4096]{1,0:T(8,128)(2,1)S(1)}, ...), branch_computations={%region_3.3_spmd, %region_4.6_spmd} | conditional | flops 67970560 | bytes 14764648 | solution.py:140
  252.5 8.9 %conditional.4 = (bf16[16,4096]{1,0:T(8,128)(2,1)}, bf16[16,4096]{1,0:T(8,128)(2,1)S(1)}, bf16[16,128]{1,0:T(8,128)(2,1)}, bf16[16,128]{1,0:T(8,128)(2,1)S(1)}, ...) conditional(s32[]{:T(128)} %convert_element_type.174, () %tuple.109, (bf16[16,4096]{1,0:T(8,128)(2,1)S(1)}, ...), branch_computations={%region_3.3_spmd, %region_4.6_spmd} | conditional | flops 67970560 | bytes 14764648 | solution.py:140
  324.3 241.3 %while.50 = (s32[]{:T(128)}, bf16[16,4096]{1,0:T(8,128)(2,1)S(1)}, bf16[8,16,4096]{2,1,0:T(8,128)(2,1)}, bf16[8,16,128]{2,1,0:T(8,128)(2,1)}, bf16[8,16,128]{2,1...) while((s32[]{:T(128)}, bf16[16,4096]{1,0:T(8,128)(2,1)S(1)}, ...), condition=%wide.region_15.16_spmd, body=%wide.region_8.15_spmd.sunk | while | flops 68961784 | bytes 9356268 | solution.py:192
  353.5 33.2 %collective-permute-done.1 = bf16[16,4096]{1,0:T(8,128)(2,1)S(1)} collective-permute-done((bf16[16,4096]{1,0:T(8,128)(2,1)}, bf16[16,4096]{1,0:T(8,128)(2,1)S(1)}, u32[]{:S(2)}, u32[]{:S(2)}) %collective-permute-start.1) | collective-permute-done | bytes 131104 | tf_op jit(solution)/shard_map/while/body/eval_jaxpr/ppermute | solution.py:14
  386.7 13.7 %conditional.5 = (bf16[16,4096]{1,0:T(8,128)(2,1)}, bf16[16,4096]{1,0:T(8,128)(2,1)S(1)}, bf16[16,128]{1,0:T(8,128)(2,1)S(1)}, bf16[16,128]{1,0:T(8,128)(2,1)}, bf16[16,128]{1,0:T(8,128)(2,1)}) conditional(s32[]{:T(128)} %convert_element_type.175, () %tuple.113, (pred[]{:T(512)}, bf16[8,16,4096]{2,1,0:T(8,128)(2,1)}, s32[]{:T(128)}, ...), branch_computations={%region_9.9_spmd, %region_10.14_spmd} | conditional | flops 68890096 | bytes 8113206 | solution.py:175
  409.1 13.7 %conditional.5 = (bf16[16,4096]{1,0:T(8,128)(2,1)}, bf16[16,4096]{1,0:T(8,128)(2,1)S(1)}, bf16[16,128]{1,0:T(8,128)(2,1)S(1)}, bf16[16,128]{1,0:T(8,128)(2,1)}, bf16[16,128]{1,0:T(8,128)(2,1)}) conditional(s32[]{:T(128)} %convert_element_type.175, () %tuple.113, (pred[]{:T(512)}, bf16[8,16,4096]{2,1,0:T(8,128)(2,1)}, s32[]{:T(128)}, ...), branch_computations={%region_9.9_spmd, %region_10.14_spmd} | conditional | flops 68890096 | bytes 8113206 | solution.py:175
  431.6 13.7 %conditional.5 = (bf16[16,4096]{1,0:T(8,128)(2,1)}, bf16[16,4096]{1,0:T(8,128)(2,1)S(1)}, bf16[16,128]{1,0:T(8,128)(2,1)S(1)}, bf16[16,128]{1,0:T(8,128)(2,1)}, bf16[16,128]{1,0:T(8,128)(2,1)}) conditional(s32[]{:T(128)} %convert_element_type.175, () %tuple.113, (pred[]{:T(512)}, bf16[8,16,4096]{2,1,0:T(8,128)(2,1)}, s32[]{:T(128)}, ...), branch_computations={%region_9.9_spmd, %region_10.14_spmd} | conditional | flops 68890096 | bytes 8113206 | solution.py:175
  454.0 13.7 %conditional.5 = (bf16[16,4096]{1,0:T(8,128)(2,1)}, bf16[16,4096]{1,0:T(8,128)(2,1)S(1)}, bf16[16,128]{1,0:T(8,128)(2,1)S(1)}, bf16[16,128]{1,0:T(8,128)(2,1)}, bf16[16,128]{1,0:T(8,128)(2,1)}) conditional(s32[]{:T(128)} %convert_element_type.175, () %tuple.113, (pred[]{:T(512)}, bf16[8,16,4096]{2,1,0:T(8,128)(2,1)}, s32[]{:T(128)}, ...), branch_computations={%region_9.9_spmd, %region_10.14_spmd} | conditional | flops 68890096 | bytes 8113206 | solution.py:175
  476.4 13.7 %conditional.5 = (bf16[16,4096]{1,0:T(8,128)(2,1)}, bf16[16,4096]{1,0:T(8,128)(2,1)S(1)}, bf16[16,128]{1,0:T(8,128)(2,1)S(1)}, bf16[16,128]{1,0:T(8,128)(2,1)}, bf16[16,128]{1,0:T(8,128)(2,1)}) conditional(s32[]{:T(128)} %convert_element_type.175, () %tuple.113, (pred[]{:T(512)}, bf16[8,16,4096]{2,1,0:T(8,128)(2,1)}, s32[]{:T(128)}, ...), branch_computations={%region_9.9_spmd, %region_10.14_spmd} | conditional | flops 68890096 | bytes 8113206 | solution.py:175
  498.9 13.7 %conditional.5 = (bf16[16,4096]{1,0:T(8,128)(2,1)}, bf16[16,4096]{1,0:T(8,128)(2,1)S(1)}, bf16[16,128]{1,0:T(8,128)(2,1)S(1)}, bf16[16,128]{1,0:T(8,128)(2,1)}, bf16[16,128]{1,0:T(8,128)(2,1)}) conditional(s32[]{:T(128)} %convert_element_type.175, () %tuple.113, (pred[]{:T(512)}, bf16[8,16,4096]{2,1,0:T(8,128)(2,1)}, s32[]{:T(128)}, ...), branch_computations={%region_9.9_spmd, %region_10.14_spmd} | conditional | flops 68890096 | bytes 8113206 | solution.py:175
  521.3 13.7 %conditional.5 = (bf16[16,4096]{1,0:T(8,128)(2,1)}, bf16[16,4096]{1,0:T(8,128)(2,1)S(1)}, bf16[16,128]{1,0:T(8,128)(2,1)S(1)}, bf16[16,128]{1,0:T(8,128)(2,1)}, bf16[16,128]{1,0:T(8,128)(2,1)}) conditional(s32[]{:T(128)} %convert_element_type.175, () %tuple.113, (pred[]{:T(512)}, bf16[8,16,4096]{2,1,0:T(8,128)(2,1)}, s32[]{:T(128)}, ...), branch_computations={%region_9.9_spmd, %region_10.14_spmd} | conditional | flops 68890096 | bytes 8113206 | solution.py:175
  543.7 13.7 %conditional.5 = (bf16[16,4096]{1,0:T(8,128)(2,1)}, bf16[16,4096]{1,0:T(8,128)(2,1)S(1)}, bf16[16,128]{1,0:T(8,128)(2,1)S(1)}, bf16[16,128]{1,0:T(8,128)(2,1)}, bf16[16,128]{1,0:T(8,128)(2,1)}) conditional(s32[]{:T(128)} %convert_element_type.175, () %tuple.113, (pred[]{:T(512)}, bf16[8,16,4096]{2,1,0:T(8,128)(2,1)}, s32[]{:T(128)}, ...), branch_computations={%region_9.9_spmd, %region_10.14_spmd} | conditional | flops 68890096 | bytes 8113206 | solution.py:175
  576.0 96.0 %all-reduce.3.cloned.1.call-done = (bf16[4096,128]{1,0:T(8,128)(2,1)}, bf16[4096,128]{1,0:T(8,128)(2,1)}, bf16[4096,128]{1,0:T(8,128)(2,1)}, bf16[4096,128]{1,0:T(8,128)(2,1)}) async-done(((bf16[4096,128]{1,0:T(8,128)(2,1)}, bf16[4096,128]{1,0:T(8,128)(2,1)}, bf16[4096,128]{1,0:T(8,128)(2,1)}, bf16[4096,128]{1,0:T(8,128)(2,1)}), (bf16[4096,128]{1,0:T(8,128)(2,1)}, bf16[4096,128]{1,0:T(8,128)(2,1)}, ...) | async-done | bytes 4194320 | tf_op jit(solution)/shard_map/psum | solution.py:201
  (669 shorter events, 457.6 us)
Async XLA Ops:
  7.2 27.5 %all-gather.9.cloned.1.call-start = ((), (), s32[]{:S(2)}) async-start(), calls=%async_computation | async-start | bytes 1179648 | tf_op jit(solution)/shard_map/all_gather | solution.py:110
  7.9 50.2 %all-gather.11.cloned.1.call-start = ((), (), s32[]{:S(2)}) async-start(), calls=%async_computation.1 | async-start | bytes 1179648 | tf_op jit(solution)/shard_map/all_gather | solution.py:111
  8.7 72.9 %all-gather.13.cloned.1.call-start = ((), (), s32[]{:S(2)}) async-start(), calls=%async_computation.2 | async-start | bytes 1179648 | tf_op jit(solution)/shard_map/all_gather | solution.py:112
  9.4 95.5 %all-gather.15.cloned.1.call-start = ((), (), s32[]{:S(2)}) async-start(), calls=%async_computation.3 | async-start | bytes 1179648 | tf_op jit(solution)/shard_map/all_gather | solution.py:113
  10.0 661.9 %all-reduce.3.cloned.1.call-start = ((), (), s32[]{:S(2)}) async-start(), calls=%async_computation.4 | async-start | bytes 8388608 | tf_op jit(solution)/shard_map/psum | solution.py:201
  140.7 8.2 %collective-permute-start = (bf16[16,4096]{1,0:T(8,128)(2,1)}, bf16[16,4096]{1,0:T(8,128)(2,1)S(1)}, u32[]{:S(2)}, u32[]{:S(2)}) collective-permute-start(bf16[16,4096]{1,0:T(8,128)(2,1)} %get-tuple-element.1244), channel_id=1, source_target_pairs={{0,8},{8,16},{16,24},{1,9},{9,17},{17,25},{2,10},{10,18},{18,26},{... | collective-permute-start | bytes 393224 | tf_op jit(solution)/shard_map/while/body/eval_jaxpr/ppermute | solution.py:14
  160.3 8.6 %collective-permute-start = (bf16[16,4096]{1,0:T(8,128)(2,1)}, bf16[16,4096]{1,0:T(8,128)(2,1)S(1)}, u32[]{:S(2)}, u32[]{:S(2)}) collective-permute-start(bf16[16,4096]{1,0:T(8,128)(2,1)} %get-tuple-element.1244), channel_id=1, source_target_pairs={{0,8},{8,16},{16,24},{1,9},{9,17},{17,25},{2,10},{10,18},{18,26},{... | collective-permute-start | bytes 393224 | tf_op jit(solution)/shard_map/while/body/eval_jaxpr/ppermute | solution.py:14
  180.3 8.9 %collective-permute-start = (bf16[16,4096]{1,0:T(8,128)(2,1)}, bf16[16,4096]{1,0:T(8,128)(2,1)S(1)}, u32[]{:S(2)}, u32[]{:S(2)}) collective-permute-start(bf16[16,4096]{1,0:T(8,128)(2,1)} %get-tuple-element.1244), channel_id=1, source_target_pairs={{0,8},{8,16},{16,24},{1,9},{9,17},{17,25},{2,10},{10,18},{18,26},{... | collective-permute-start | bytes 393224 | tf_op jit(solution)/shard_map/while/body/eval_jaxpr/ppermute | solution.py:14
  200.6 8.8 %collective-permute-start = (bf16[16,4096]{1,0:T(8,128)(2,1)}, bf16[16,4096]{1,0:T(8,128)(2,1)S(1)}, u32[]{:S(2)}, u32[]{:S(2)}) collective-permute-start(bf16[16,4096]{1,0:T(8,128)(2,1)} %get-tuple-element.1244), channel_id=1, source_target_pairs={{0,8},{8,16},{16,24},{1,9},{9,17},{17,25},{2,10},{10,18},{18,26},{... | collective-permute-start | bytes 393224 | tf_op jit(solution)/shard_map/while/body/eval_jaxpr/ppermute | solution.py:14
  220.9 8.8 %collective-permute-start = (bf16[16,4096]{1,0:T(8,128)(2,1)}, bf16[16,4096]{1,0:T(8,128)(2,1)S(1)}, u32[]{:S(2)}, u32[]{:S(2)}) collective-permute-start(bf16[16,4096]{1,0:T(8,128)(2,1)} %get-tuple-element.1244), channel_id=1, source_target_pairs={{0,8},{8,16},{16,24},{1,9},{9,17},{17,25},{2,10},{10,18},{18,26},{... | collective-permute-start | bytes 393224 | tf_op jit(solution)/shard_map/while/body/eval_jaxpr/ppermute | solution.py:14
  241.1 8.9 %collective-permute-start = (bf16[16,4096]{1,0:T(8,128)(2,1)}, bf16[16,4096]{1,0:T(8,128)(2,1)S(1)}, u32[]{:S(2)}, u32[]{:S(2)}) collective-permute-start(bf16[16,4096]{1,0:T(8,128)(2,1)} %get-tuple-element.1244), channel_id=1, source_target_pairs={{0,8},{8,16},{16,24},{1,9},{9,17},{17,25},{2,10},{10,18},{18,26},{... | collective-permute-start | bytes 393224 | tf_op jit(solution)/shard_map/while/body/eval_jaxpr/ppermute | solution.py:14
  261.4 8.8 %collective-permute-start = (bf16[16,4096]{1,0:T(8,128)(2,1)}, bf16[16,4096]{1,0:T(8,128)(2,1)S(1)}, u32[]{:S(2)}, u32[]{:S(2)}) collective-permute-start(bf16[16,4096]{1,0:T(8,128)(2,1)} %get-tuple-element.1244), channel_id=1, source_target_pairs={{0,8},{8,16},{16,24},{1,9},{9,17},{17,25},{2,10},{10,18},{18,26},{... | collective-permute-start | bytes 393224 | tf_op jit(solution)/shard_map/while/body/eval_jaxpr/ppermute | solution.py:14
  275.2 13.9 %collective-permute-start = (bf16[16,4096]{1,0:T(8,128)(2,1)}, bf16[16,4096]{1,0:T(8,128)(2,1)S(1)}, u32[]{:S(2)}, u32[]{:S(2)}) collective-permute-start(bf16[16,4096]{1,0:T(8,128)(2,1)} %get-tuple-element.1244), channel_id=1, source_target_pairs={{0,8},{8,16},{16,24},{1,9},{9,17},{17,25},{2,10},{10,18},{18,26},{... | collective-permute-start | bytes 393224 | tf_op jit(solution)/shard_map/while/body/eval_jaxpr/ppermute | solution.py:14
  294.1 8.8 %collective-permute-start = (bf16[16,4096]{1,0:T(8,128)(2,1)}, bf16[16,4096]{1,0:T(8,128)(2,1)S(1)}, u32[]{:S(2)}, u32[]{:S(2)}) collective-permute-start(bf16[16,4096]{1,0:T(8,128)(2,1)} %get-tuple-element.1244), channel_id=1, source_target_pairs={{0,8},{8,16},{16,24},{1,9},{9,17},{17,25},{2,10},{10,18},{18,26},{... | collective-permute-start | bytes 393224 | tf_op jit(solution)/shard_map/while/body/eval_jaxpr/ppermute | solution.py:14
  308.0 13.4 %collective-permute-start = (bf16[16,4096]{1,0:T(8,128)(2,1)}, bf16[16,4096]{1,0:T(8,128)(2,1)S(1)}, u32[]{:S(2)}, u32[]{:S(2)}) collective-permute-start(bf16[16,4096]{1,0:T(8,128)(2,1)} %get-tuple-element.1244), channel_id=1, source_target_pairs={{0,8},{8,16},{16,24},{1,9},{9,17},{17,25},{2,10},{10,18},{18,26},{... | collective-permute-start | bytes 393224 | tf_op jit(solution)/shard_map/while/body/eval_jaxpr/ppermute | solution.py:14
  335.5 8.7 %collective-permute-start.1 = (bf16[16,4096]{1,0:T(8,128)(2,1)}, bf16[16,4096]{1,0:T(8,128)(2,1)S(1)}, u32[]{:S(2)}, u32[]{:S(2)}) collective-permute-start(bf16[16,4096]{1,0:T(8,128)(2,1)} %get-tuple-element.1274), channel_id=1, source_target_pairs={{8,0},{16,8},{24,16},{9,1},{17,9},{25,17},{10,2},{18,10},{26,18},{... | collective-permute-start | bytes 393224 | tf_op jit(solution)/shard_map/while/body/eval_jaxpr/ppermute | solution.py:14
  346.1 40.6 %collective-permute-start.1 = (bf16[16,4096]{1,0:T(8,128)(2,1)}, bf16[16,4096]{1,0:T(8,128)(2,1)S(1)}, u32[]{:S(2)}, u32[]{:S(2)}) collective-permute-start(bf16[16,4096]{1,0:T(8,128)(2,1)} %get-tuple-element.1274), channel_id=1, source_target_pairs={{8,0},{16,8},{24,16},{9,1},{17,9},{25,17},{10,2},{18,10},{26,18},{... | collective-permute-start | bytes 393224 | tf_op jit(solution)/shard_map/while/body/eval_jaxpr/ppermute | solution.py:14
  400.4 8.7 %collective-permute-start.1 = (bf16[16,4096]{1,0:T(8,128)(2,1)}, bf16[16,4096]{1,0:T(8,128)(2,1)S(1)}, u32[]{:S(2)}, u32[]{:S(2)}) collective-permute-start(bf16[16,4096]{1,0:T(8,128)(2,1)} %get-tuple-element.1274), channel_id=1, source_target_pairs={{8,0},{16,8},{24,16},{9,1},{17,9},{25,17},{10,2},{18,10},{26,18},{... | collective-permute-start | bytes 393224 | tf_op jit(solution)/shard_map/while/body/eval_jaxpr/ppermute | solution.py:14
  422.8 8.7 %collective-permute-start.1 = (bf16[16,4096]{1,0:T(8,128)(2,1)}, bf16[16,4096]{1,0:T(8,128)(2,1)S(1)}, u32[]{:S(2)}, u32[]{:S(2)}) collective-permute-start(bf16[16,4096]{1,0:T(8,128)(2,1)} %get-tuple-element.1274), channel_id=1, source_target_pairs={{8,0},{16,8},{24,16},{9,1},{17,9},{25,17},{10,2},{18,10},{26,18},{... | collective-permute-start | bytes 393224 | tf_op jit(solution)/shard_map/while/body/eval_jaxpr/ppermute | solution.py:14
  445.3 8.7 %collective-permute-start.1 = (bf16[16,4096]{1,0:T(8,128)(2,1)}, bf16[16,4096]{1,0:T(8,128)(2,1)S(1)}, u32[]{:S(2)}, u32[]{:S(2)}) collective-permute-start(bf16[16,4096]{1,0:T(8,128)(2,1)} %get-tuple-element.1274), channel_id=1, source_target_pairs={{8,0},{16,8},{24,16},{9,1},{17,9},{25,17},{10,2},{18,10},{26,18},{... | collective-permute-start | bytes 393224 | tf_op jit(solution)/shard_map/while/body/eval_jaxpr/ppermute | solution.py:14
  467.7 8.7 %collective-permute-start.1 = (bf16[16,4096]{1,0:T(8,128)(2,1)}, bf16[16,4096]{1,0:T(8,128)(2,1)S(1)}, u32[]{:S(2)}, u32[]{:S(2)}) collective-permute-start(bf16[16,4096]{1,0:T(8,128)(2,1)} %get-tuple-element.1274), channel_id=1, source_target_pairs={{8,0},{16,8},{24,16},{9,1},{17,9},{25,17},{10,2},{18,10},{26,18},{... | collective-permute-start | bytes 393224 | tf_op jit(solution)/shard_map/while/body/eval_jaxpr/ppermute | solution.py:14
  490.1 8.7 %collective-permute-start.1 = (bf16[16,4096]{1,0:T(8,128)(2,1)}, bf16[16,4096]{1,0:T(8,128)(2,1)S(1)}, u32[]{:S(2)}, u32[]{:S(2)}) collective-permute-start(bf16[16,4096]{1,0:T(8,128)(2,1)} %get-tuple-element.1274), channel_id=1, source_target_pairs={{8,0},{16,8},{24,16},{9,1},{17,9},{25,17},{10,2},{18,10},{26,18},{... | collective-permute-start | bytes 393224 | tf_op jit(solution)/shard_map/while/body/eval_jaxpr/ppermute | solution.py:14
  512.6 8.7 %collective-permute-start.1 = (bf16[16,4096]{1,0:T(8,128)(2,1)}, bf16[16,4096]{1,0:T(8,128)(2,1)S(1)}, u32[]{:S(2)}, u32[]{:S(2)}) collective-permute-start(bf16[16,4096]{1,0:T(8,128)(2,1)} %get-tuple-element.1274), channel_id=1, source_target_pairs={{8,0},{16,8},{24,16},{9,1},{17,9},{25,17},{10,2},{18,10},{26,18},{... | collective-permute-start | bytes 393224 | tf_op jit(solution)/shard_map/while/body/eval_jaxpr/ppermute | solution.py:14
  535.0 8.7 %collective-permute-start.1 = (bf16[16,4096]{1,0:T(8,128)(2,1)}, bf16[16,4096]{1,0:T(8,128)(2,1)S(1)}, u32[]{:S(2)}, u32[]{:S(2)}) collective-permute-start(bf16[16,4096]{1,0:T(8,128)(2,1)} %get-tuple-element.1274), channel_id=1, source_target_pairs={{8,0},{16,8},{24,16},{9,1},{17,9},{25,17},{10,2},{18,10},{26,18},{... | collective-permute-start | bytes 393224 | tf_op jit(solution)/shard_map/while/body/eval_jaxpr/ppermute | solution.py:14
  (90 other events, 321.1 us)
Sparse Core Ops, SparseCore 0:
  9.6 25.0 all-gather.8
  36.2 21.8 all-gather.10
  59.7 21.8 all-gather.12
  83.1 21.8 all-gather.14
  576.1 95.7 all-reduce.2
where the time goes:
time: 691 us; the launch traced here: 682 us
  waiting for transfers between devices  231 us (33%)
  matrix products  135 us (20%)
  local copies, waits for them, and re-layouts  130 us (19%)
  other arithmetic  124 us (18%)
  starting transfers between devices  47.5 us (7%)
  between operations  13.8 us (2%)
    psum x1, waiting for transfers between devices, on_device(): lax.psum(full_q.astype(jnp.bfloat16), 'rep').astype(jnp.float32)  96 us
    dynamic_slice x110, local copies, waits for them, and re-layouts, store_slot(): old_value = lax.dynamic_index_in_dim(store, slot_at, 0, keepdims=False)  89.3 us
    dynamic_update_slice x77, other arithmetic, store_slot(): return lax.dynamic_update_index_in_dim(store, fresh, slot_at, 0)  83.6 us
    ppermute x22, starting transfers between devices, from_behind(): return lax.ppermute(block, axis, route)  47.3 us
    ppermute x22, waiting for transfers between devices, from_behind(): return lax.ppermute(block, axis, route)  38.9 us
    all_gather x1, waiting for transfers between devices, on_device(): lax.all_gather(w_v[0], 'rep', axis=0, tiled=True)  23.5 us
    all_gather x1, waiting for transfers between devices, on_device(): lax.all_gather(w_k[0], 'rep', axis=0, tiled=True)  23.5 us
    all_gather x1, waiting for transfers between devices, on_device(): lax.all_gather(w_out[0], 'rep', axis=0, tiled=True)  23.3 us
  transfers between devices with their start and end apart: 27, of which 14 were waited for; matrix products, arithmetic and copies ran while one was open for 21% of the time, Pallas kernels for 0%

commit v1 on v0

--- a/solution.py
+++ b/solution.py
@@ -198,7 +198,7 @@
     full_o = local_grad(saved_rows, saved_heads)
     share_width = width // rep_count
     totals = (
-        lax.psum(full_q.astype(jnp.bfloat16), "rep").astype(jnp.float32),
+        jnp.sum(lax.all_gather(full_q.astype(jnp.bfloat16), "rep"), axis=0).astype(jnp.float32),
         lax.psum(full_k.astype(jnp.bfloat16), "rep").astype(jnp.float32),
         lax.psum(full_v.astype(jnp.bfloat16), "rep").astype(jnp.float32),
         lax.psum(full_o.astype(jnp.bfloat16), "rep").astype(jnp.float32),

time: 691 us -> 790 us (1.14)
  waiting for transfers between devices: 231 us -> 297 us
  matrix products: 135 us -> 165 us
  local copies, waits for them, and re-layouts: 130 us -> 121 us
    all_gather x0 -> x1, waiting for transfers between devices: none -> 80.1 us  [on_device(): lax.all_gather(full_q.astype(jnp.bfloat16), 'rep')]
    psum x1, waiting for transfers between devices: 96 us -> 73.4 us  [on_device(): lax.psum(full_k.astype(jnp.bfloat16), 'rep').astype(jnp.float32)]
    dot_general x8, matrix products: 1.99 us -> 14 us  [forward_layer(): jnp.dot(normed, weight_k, preferred_element_type=jnp.float32)]
    dynamic_slice x110, local copies, waits for them, and re-layouts: 89.3 us -> 79.5 us  [store_slot(): old_value = lax.dynamic_index_in_dim(store, slot_at, 0, keepdims=False)]
    ppermute x22, waiting for transfers between devices: 38.9 us -> 47.3 us  [from_behind(): return lax.ppermute(block, axis, route)]
  transfers between devices with their start and end apart: 27 -> 28, of which waited for: 14 -> 16; matrix products, arithmetic and copies ran while one was open for 21% -> 18% of each run, Pallas kernels for 0% -> 0%
where the time goes in v1:
time: 790 us; the launch traced here: 781 us
  waiting for transfers between devices  297 us (38%)
  matrix products  165 us (21%)
  other arithmetic  130 us (16%)
  local copies, waits for them, and re-layouts  121 us (15%)
  starting transfers between devices  53.1 us (7%)
  between operations  14.2 us (2%)
    dynamic_update_slice x77, other arithmetic, store_slot(): return lax.dynamic_update_index_in_dim(store, fresh, slot_at, 0)  83.7 us
    all_gather x1, waiting for transfers between devices, on_device(): lax.all_gather(full_q.astype(jnp.bfloat16), 'rep')  80.1 us
    dynamic_slice x110, local copies, waits for them, and re-layouts, store_slot(): old_value = lax.dynamic_index_in_dim(store, slot_at, 0, keepdims=False)  79.5 us
    psum x1, waiting for transfers between devices, on_device(): lax.psum(full_k.astype(jnp.bfloat16), 'rep').astype(jnp.float32)  73.4 us
    ppermute x22, starting transfers between devices, from_behind(): return lax.ppermute(block, axis, route)  52.8 us
    ppermute x22, waiting for transfers between devices, from_behind(): return lax.ppermute(block, axis, route)  47.3 us
    all_gather x1, waiting for transfers between devices, on_device(): lax.all_gather(w_v[0], 'rep', axis=0, tiled=True)  23.5 us
    all_gather x1, waiting for transfers between devices, on_device(): lax.all_gather(w_k[0], 'rep', axis=0, tiled=True)  23.5 us
  transfers between devices with their start and end apart: 28, of which 16 were waited for; matrix products, arithmetic and copies ran while one was open for 18% of the time, Pallas kernels for 0%

profile of v1, /device:TPU:0, one launch (start us, length us, event | category | flops | bytes accessed | tf_op | source)
XLA Modules:
  0.0 780.9 jit_solution(3889571451791571729)
XLA Ops:
  11.5 23.2 %all-gather.11.cloned.1.call-done = bf16[1,4096,128]{2,1,0:T(8,128)(2,1)} async-done(((bf16[1,512,128]{2,1,0:T(8,128)(2,1)}), bf16[1,4096,128]{2,1,0:T(8,128)(2,1)}) %all-gather.11.cloned.1.call-update) | async-done | bytes 1048592 | tf_op jit(solution)/shard_map/all_gather | solution.py:110
  34.6 23.5 %all-gather.13.cloned.1.call-done = bf16[1,4096,128]{2,1,0:T(8,128)(2,1)} async-done(((bf16[1,512,128]{2,1,0:T(8,128)(2,1)}), bf16[1,4096,128]{2,1,0:T(8,128)(2,1)}) %all-gather.13.cloned.1.call-update) | async-done | bytes 1048592 | tf_op jit(solution)/shard_map/all_gather | solution.py:111
  58.1 23.5 %all-gather.15.cloned.1.call-done = bf16[1,4096,128]{2,1,0:T(8,128)(2,1)} async-done(((bf16[1,512,128]{2,1,0:T(8,128)(2,1)}), bf16[1,4096,128]{2,1,0:T(8,128)(2,1)}) %all-gather.15.cloned.1.call-update) | async-done | bytes 1048592 | tf_op jit(solution)/shard_map/all_gather | solution.py:112
  81.6 23.3 %all-gather.17.cloned.1.call-done = bf16[1,4096,128]{2,1,0:T(8,128)(2,1)} async-done(((bf16[1,512,128]{2,1,0:T(8,128)(2,1)}), bf16[1,4096,128]{2,1,0:T(8,128)(2,1)}) %all-gather.17.cloned.1.call-update) | async-done | bytes 1048592 | tf_op jit(solution)/shard_map/all_gather | solution.py:113
  108.6 244.8 %while.49 = (s32[]{:T(128)}, bf16[16,4096]{1,0:T(8,128)(2,1)S(1)}, bf16[8,16,4096]{2,1,0:T(8,128)(2,1)}, bf16[8,16,4096]{2,1,0:T(8,128)(2,1)S(1)}, bf16[8,16,128...) while((s32[]{:T(128)}, bf16[16,4096]{1,0:T(8,128)(2,1)S(1)}, ...), condition=%wide.region_7.8_spmd, body=%wide.region_2.7_spmd.sunk | while | flops 68175368 | bytes 15864699 | solution.py:159
  111.1 12.2 %conditional.4 = (bf16[16,4096]{1,0:T(8,128)(2,1)S(1)}, bf16[16,4096]{1,0:T(8,128)(2,1)}, bf16[16,128]{1,0:T(8,128)(2,1)}, bf16[16,128]{1,0:T(8,128)(2,1)}, bf16...) conditional(s32[]{:T(128)} %convert_element_type.176, () %tuple.108, (bf16[16,4096]{1,0:T(8,128)(2,1)S(1)}, ...), branch_computations={%region_3.3_spmd, %region_4.6_spmd} | conditional | flops 67970560 | bytes 13683192 | solution.py:140
  134.1 12.2 %conditional.4 = (bf16[16,4096]{1,0:T(8,128)(2,1)S(1)}, bf16[16,4096]{1,0:T(8,128)(2,1)}, bf16[16,128]{1,0:T(8,128)(2,1)}, bf16[16,128]{1,0:T(8,128)(2,1)}, bf16...) conditional(s32[]{:T(128)} %convert_element_type.176, () %tuple.108, (bf16[16,4096]{1,0:T(8,128)(2,1)S(1)}, ...), branch_computations={%region_3.3_spmd, %region_4.6_spmd} | conditional | flops 67970560 | bytes 13683192 | solution.py:140
  157.1 12.2 %conditional.4 = (bf16[16,4096]{1,0:T(8,128)(2,1)S(1)}, bf16[16,4096]{1,0:T(8,128)(2,1)}, bf16[16,128]{1,0:T(8,128)(2,1)}, bf16[16,128]{1,0:T(8,128)(2,1)}, bf16...) conditional(s32[]{:T(128)} %convert_element_type.176, () %tuple.108, (bf16[16,4096]{1,0:T(8,128)(2,1)S(1)}, ...), branch_computations={%region_3.3_spmd, %region_4.6_spmd} | conditional | flops 67970560 | bytes 13683192 | solution.py:140
  180.3 12.2 %conditional.4 = (bf16[16,4096]{1,0:T(8,128)(2,1)S(1)}, bf16[16,4096]{1,0:T(8,128)(2,1)}, bf16[16,128]{1,0:T(8,128)(2,1)}, bf16[16,128]{1,0:T(8,128)(2,1)}, bf16...) conditional(s32[]{:T(128)} %convert_element_type.176, () %tuple.108, (bf16[16,4096]{1,0:T(8,128)(2,1)S(1)}, ...), branch_computations={%region_3.3_spmd, %region_4.6_spmd} | conditional | flops 67970560 | bytes 13683192 | solution.py:140
  203.8 12.2 %conditional.4 = (bf16[16,4096]{1,0:T(8,128)(2,1)S(1)}, bf16[16,4096]{1,0:T(8,128)(2,1)}, bf16[16,128]{1,0:T(8,128)(2,1)}, bf16[16,128]{1,0:T(8,128)(2,1)}, bf16...) conditional(s32[]{:T(128)} %convert_element_type.176, () %tuple.108, (bf16[16,4096]{1,0:T(8,128)(2,1)S(1)}, ...), branch_computations={%region_3.3_spmd, %region_4.6_spmd} | conditional | flops 67970560 | bytes 13683192 | solution.py:140
  227.5 12.2 %conditional.4 = (bf16[16,4096]{1,0:T(8,128)(2,1)S(1)}, bf16[16,4096]{1,0:T(8,128)(2,1)}, bf16[16,128]{1,0:T(8,128)(2,1)}, bf16[16,128]{1,0:T(8,128)(2,1)}, bf16...) conditional(s32[]{:T(128)} %convert_element_type.176, () %tuple.108, (bf16[16,4096]{1,0:T(8,128)(2,1)S(1)}, ...), branch_computations={%region_3.3_spmd, %region_4.6_spmd} | conditional | flops 67970560 | bytes 13683192 | solution.py:140
  251.0 12.2 %conditional.4 = (bf16[16,4096]{1,0:T(8,128)(2,1)S(1)}, bf16[16,4096]{1,0:T(8,128)(2,1)}, bf16[16,128]{1,0:T(8,128)(2,1)}, bf16[16,128]{1,0:T(8,128)(2,1)}, bf16...) conditional(s32[]{:T(128)} %convert_element_type.176, () %tuple.108, (bf16[16,4096]{1,0:T(8,128)(2,1)S(1)}, ...), branch_computations={%region_3.3_spmd, %region_4.6_spmd} | conditional | flops 67970560 | bytes 13683192 | solution.py:140
  356.5 245.9 %while.50 = (s32[]{:T(128)}, bf16[16,4096]{1,0:T(8,128)(2,1)S(1)}, bf16[8,16,4096]{2,1,0:T(8,128)(2,1)}, bf16[8,16,128]{2,1,0:T(8,128)(2,1)}, bf16[8,16,128]{2,1...) while((s32[]{:T(128)}, bf16[16,4096]{1,0:T(8,128)(2,1)S(1)}, ...), condition=%wide.region_15.16_spmd, body=%wide.region_8.15_spmd.sunk | while | flops 68961784 | bytes 13517776 | solution.py:192
  386.5 36.7 %collective-permute-done.1 = bf16[16,4096]{1,0:T(8,128)(2,1)S(1)} collective-permute-done((bf16[16,4096]{1,0:T(8,128)(2,1)S(1)}, bf16[16,4096]{1,0:T(8,128)(2,1)S(1)}, u32[]{:S(2)}, u32[]{:S(2)}) %collective-permute-start.1) | collective-permute-done | bytes 131104 | tf_op jit(solution)/shard_map/while/body/eval_jaxpr/ppermute | solution.py:14
  423.2 14.3 %conditional.5 = (bf16[16,4096]{1,0:T(8,128)(2,1)S(1)}, bf16[16,4096]{1,0:T(8,128)(2,1)S(1)}, bf16[16,128]{1,0:T(8,128)(2,1)}, bf16[16,128]{1,0:T(8,128)(2,1)}, bf16[16,128]{1,0:T(8,128)(2,1)}) conditional(s32[]{:T(128)} %convert_element_type.177, () %tuple.112, (pred[]{:T(512)}, bf16[8,16,4096]{2,1,0:T(8,128)(2,1)}, s32[]{:T(128)}, ...), branch_computations={%region_9.9_spmd, %region_10.14_spmd} | conditional | flops 68890096 | bytes 12274714 | solution.py:175
  445.7 14.3 %conditional.5 = (bf16[16,4096]{1,0:T(8,128)(2,1)S(1)}, bf16[16,4096]{1,0:T(8,128)(2,1)S(1)}, bf16[16,128]{1,0:T(8,128)(2,1)}, bf16[16,128]{1,0:T(8,128)(2,1)}, bf16[16,128]{1,0:T(8,128)(2,1)}) conditional(s32[]{:T(128)} %convert_element_type.177, () %tuple.112, (pred[]{:T(512)}, bf16[8,16,4096]{2,1,0:T(8,128)(2,1)}, s32[]{:T(128)}, ...), branch_computations={%region_9.9_spmd, %region_10.14_spmd} | conditional | flops 68890096 | bytes 12274714 | solution.py:175
  468.2 14.3 %conditional.5 = (bf16[16,4096]{1,0:T(8,128)(2,1)S(1)}, bf16[16,4096]{1,0:T(8,128)(2,1)S(1)}, bf16[16,128]{1,0:T(8,128)(2,1)}, bf16[16,128]{1,0:T(8,128)(2,1)}, bf16[16,128]{1,0:T(8,128)(2,1)}) conditional(s32[]{:T(128)} %convert_element_type.177, () %tuple.112, (pred[]{:T(512)}, bf16[8,16,4096]{2,1,0:T(8,128)(2,1)}, s32[]{:T(128)}, ...), branch_computations={%region_9.9_spmd, %region_10.14_spmd} | conditional | flops 68890096 | bytes 12274714 | solution.py:175
  490.6 14.3 %conditional.5 = (bf16[16,4096]{1,0:T(8,128)(2,1)S(1)}, bf16[16,4096]{1,0:T(8,128)(2,1)S(1)}, bf16[16,128]{1,0:T(8,128)(2,1)}, bf16[16,128]{1,0:T(8,128)(2,1)}, bf16[16,128]{1,0:T(8,128)(2,1)}) conditional(s32[]{:T(128)} %convert_element_type.177, () %tuple.112, (pred[]{:T(512)}, bf16[8,16,4096]{2,1,0:T(8,128)(2,1)}, s32[]{:T(128)}, ...), branch_computations={%region_9.9_spmd, %region_10.14_spmd} | conditional | flops 68890096 | bytes 12274714 | solution.py:175
  513.1 14.3 %conditional.5 = (bf16[16,4096]{1,0:T(8,128)(2,1)S(1)}, bf16[16,4096]{1,0:T(8,128)(2,1)S(1)}, bf16[16,128]{1,0:T(8,128)(2,1)}, bf16[16,128]{1,0:T(8,128)(2,1)}, bf16[16,128]{1,0:T(8,128)(2,1)}) conditional(s32[]{:T(128)} %convert_element_type.177, () %tuple.112, (pred[]{:T(512)}, bf16[8,16,4096]{2,1,0:T(8,128)(2,1)}, s32[]{:T(128)}, ...), branch_computations={%region_9.9_spmd, %region_10.14_spmd} | conditional | flops 68890096 | bytes 12274714 | solution.py:175
  535.6 14.3 %conditional.5 = (bf16[16,4096]{1,0:T(8,128)(2,1)S(1)}, bf16[16,4096]{1,0:T(8,128)(2,1)S(1)}, bf16[16,128]{1,0:T(8,128)(2,1)}, bf16[16,128]{1,0:T(8,128)(2,1)}, bf16[16,128]{1,0:T(8,128)(2,1)}) conditional(s32[]{:T(128)} %convert_element_type.177, () %tuple.112, (pred[]{:T(512)}, bf16[8,16,4096]{2,1,0:T(8,128)(2,1)}, s32[]{:T(128)}, ...), branch_computations={%region_9.9_spmd, %region_10.14_spmd} | conditional | flops 68890096 | bytes 12274714 | solution.py:175
  558.1 14.3 %conditional.5 = (bf16[16,4096]{1,0:T(8,128)(2,1)S(1)}, bf16[16,4096]{1,0:T(8,128)(2,1)S(1)}, bf16[16,128]{1,0:T(8,128)(2,1)}, bf16[16,128]{1,0:T(8,128)(2,1)}, bf16[16,128]{1,0:T(8,128)(2,1)}) conditional(s32[]{:T(128)} %convert_element_type.177, () %tuple.112, (pred[]{:T(512)}, bf16[8,16,4096]{2,1,0:T(8,128)(2,1)}, s32[]{:T(128)}, ...), branch_computations={%region_9.9_spmd, %region_10.14_spmd} | conditional | flops 68890096 | bytes 12274714 | solution.py:175
  580.6 14.3 %conditional.5 = (bf16[16,4096]{1,0:T(8,128)(2,1)S(1)}, bf16[16,4096]{1,0:T(8,128)(2,1)S(1)}, bf16[16,128]{1,0:T(8,128)(2,1)}, bf16[16,128]{1,0:T(8,128)(2,1)}, bf16[16,128]{1,0:T(8,128)(2,1)}) conditional(s32[]{:T(128)} %convert_element_type.177, () %tuple.112, (pred[]{:T(512)}, bf16[8,16,4096]{2,1,0:T(8,128)(2,1)}, s32[]{:T(128)}, ...), branch_computations={%region_9.9_spmd, %region_10.14_spmd} | conditional | flops 68890096 | bytes 12274714 | solution.py:175
  611.2 73.4 %all-reduce.3.cloned.1.call-done = (bf16[4096,128]{1,0:T(8,128)(2,1)}, bf16[4096,128]{1,0:T(8,128)(2,1)}, bf16[4096,128]{1,0:T(8,128)(2,1)}) async-done(((bf16[4096,128]{1,0:T(8,128)(2,1)}, bf16[4096,128]{1,0:T(8,128)(2,1)}, bf16[4096,128]{1,0:T(8,128)(2,1)}), (bf16[4096,128]{1,0:T(8,128)(2,1)}, bf16[4096,128]{1,0:T(8,128)(2,1)}, bf16[4096,128]{1,0:T(8,128)(2,1)})) %all-reduce.3.cloned.1.call-update) | async-done | bytes 3145744 | tf_op jit(solution)/shard_map/psum | solution.py:202
  688.0 80.1 %all-gather.19.cloned.1.call-done = bf16[32768,128]{1,0:T(8,128)(2,1)} async-done(((bf16[4096,128]{1,0:T(8,128)(2,1)}), bf16[32768,128]{1,0:T(8,128)(2,1)}) %all-gather.19.cloned.1.call-update) | async-done | bytes 8388624 | tf_op jit(solution)/shard_map/all_gather | solution.py:201
  (596 shorter events, 509.0 us)
Async XLA Ops:
  7.2 27.5 %all-gather.11.cloned.1.call-start = ((), (), s32[]{:S(2)}) async-start(), calls=%async_computation | async-start | bytes 1179648 | tf_op jit(solution)/shard_map/all_gather | solution.py:110
  7.9 50.2 %all-gather.13.cloned.1.call-start = ((), (), s32[]{:S(2)}) async-start(), calls=%async_computation.1 | async-start | bytes 1179648 | tf_op jit(solution)/shard_map/all_gather | solution.py:111
  8.7 72.9 %all-gather.15.cloned.1.call-start = ((), (), s32[]{:S(2)}) async-start(), calls=%async_computation.2 | async-start | bytes 1179648 | tf_op jit(solution)/shard_map/all_gather | solution.py:112
  9.4 95.5 %all-gather.17.cloned.1.call-start = ((), (), s32[]{:S(2)}) async-start(), calls=%async_computation.3 | async-start | bytes 1179648 | tf_op jit(solution)/shard_map/all_gather | solution.py:113
  10.0 674.6 %all-reduce.3.cloned.1.call-start = ((), (), s32[]{:S(2)}) async-start(), calls=%async_computation.5 | async-start | bytes 6291456 | tf_op jit(solution)/shard_map/psum | solution.py:202
  123.4 8.2 %collective-permute-start = (bf16[16,4096]{1,0:T(8,128)(2,1)S(1)}, bf16[16,4096]{1,0:T(8,128)(2,1)S(1)}, u32[]{:S(2)}, u32[]{:S(2)}) collective-permute-start(bf16[16,4096]{1,0:T(8,128)(2,1)S(1)} %get-tuple-element.1241), channel_id=1, source_target_pairs={{0,8},{8,16},{16,24},{1,9},{9,17},{17,25},{2,10},{10,18},{18,26},{... | collective-permute-start | bytes 393224 | tf_op jit(solution)/shard_map/while/body/eval_jaxpr/ppermute | solution.py:14
  146.3 8.2 %collective-permute-start = (bf16[16,4096]{1,0:T(8,128)(2,1)S(1)}, bf16[16,4096]{1,0:T(8,128)(2,1)S(1)}, u32[]{:S(2)}, u32[]{:S(2)}) collective-permute-start(bf16[16,4096]{1,0:T(8,128)(2,1)S(1)} %get-tuple-element.1241), channel_id=1, source_target_pairs={{0,8},{8,16},{16,24},{1,9},{9,17},{17,25},{2,10},{10,18},{18,26},{... | collective-permute-start | bytes 393224 | tf_op jit(solution)/shard_map/while/body/eval_jaxpr/ppermute | solution.py:14
  169.3 8.4 %collective-permute-start = (bf16[16,4096]{1,0:T(8,128)(2,1)S(1)}, bf16[16,4096]{1,0:T(8,128)(2,1)S(1)}, u32[]{:S(2)}, u32[]{:S(2)}) collective-permute-start(bf16[16,4096]{1,0:T(8,128)(2,1)S(1)} %get-tuple-element.1241), channel_id=1, source_target_pairs={{0,8},{8,16},{16,24},{1,9},{9,17},{17,25},{2,10},{10,18},{18,26},{... | collective-permute-start | bytes 393224 | tf_op jit(solution)/shard_map/while/body/eval_jaxpr/ppermute | solution.py:14
  192.5 8.8 %collective-permute-start = (bf16[16,4096]{1,0:T(8,128)(2,1)S(1)}, bf16[16,4096]{1,0:T(8,128)(2,1)S(1)}, u32[]{:S(2)}, u32[]{:S(2)}) collective-permute-start(bf16[16,4096]{1,0:T(8,128)(2,1)S(1)} %get-tuple-element.1241), channel_id=1, source_target_pairs={{0,8},{8,16},{16,24},{1,9},{9,17},{17,25},{2,10},{10,18},{18,26},{... | collective-permute-start | bytes 393224 | tf_op jit(solution)/shard_map/while/body/eval_jaxpr/ppermute | solution.py:14
  216.1 8.9 %collective-permute-start = (bf16[16,4096]{1,0:T(8,128)(2,1)S(1)}, bf16[16,4096]{1,0:T(8,128)(2,1)S(1)}, u32[]{:S(2)}, u32[]{:S(2)}) collective-permute-start(bf16[16,4096]{1,0:T(8,128)(2,1)S(1)} %get-tuple-element.1241), channel_id=1, source_target_pairs={{0,8},{8,16},{16,24},{1,9},{9,17},{17,25},{2,10},{10,18},{18,26},{... | collective-permute-start | bytes 393224 | tf_op jit(solution)/shard_map/while/body/eval_jaxpr/ppermute | solution.py:14
  239.7 8.8 %collective-permute-start = (bf16[16,4096]{1,0:T(8,128)(2,1)S(1)}, bf16[16,4096]{1,0:T(8,128)(2,1)S(1)}, u32[]{:S(2)}, u32[]{:S(2)}) collective-permute-start(bf16[16,4096]{1,0:T(8,128)(2,1)S(1)} %get-tuple-element.1241), channel_id=1, source_target_pairs={{0,8},{8,16},{16,24},{1,9},{9,17},{17,25},{2,10},{10,18},{18,26},{... | collective-permute-start | bytes 393224 | tf_op jit(solution)/shard_map/while/body/eval_jaxpr/ppermute | solution.py:14
  263.2 8.9 %collective-permute-start = (bf16[16,4096]{1,0:T(8,128)(2,1)S(1)}, bf16[16,4096]{1,0:T(8,128)(2,1)S(1)}, u32[]{:S(2)}, u32[]{:S(2)}) collective-permute-start(bf16[16,4096]{1,0:T(8,128)(2,1)S(1)} %get-tuple-element.1241), channel_id=1, source_target_pairs={{0,8},{8,16},{16,24},{1,9},{9,17},{17,25},{2,10},{10,18},{18,26},{... | collective-permute-start | bytes 393224 | tf_op jit(solution)/shard_map/while/body/eval_jaxpr/ppermute | solution.py:14
  286.9 8.9 %collective-permute-start = (bf16[16,4096]{1,0:T(8,128)(2,1)S(1)}, bf16[16,4096]{1,0:T(8,128)(2,1)S(1)}, u32[]{:S(2)}, u32[]{:S(2)}) collective-permute-start(bf16[16,4096]{1,0:T(8,128)(2,1)S(1)} %get-tuple-element.1241), channel_id=1, source_target_pairs={{0,8},{8,16},{16,24},{1,9},{9,17},{17,25},{2,10},{10,18},{18,26},{... | collective-permute-start | bytes 393224 | tf_op jit(solution)/shard_map/while/body/eval_jaxpr/ppermute | solution.py:14
  301.3 16.4 %collective-permute-start = (bf16[16,4096]{1,0:T(8,128)(2,1)S(1)}, bf16[16,4096]{1,0:T(8,128)(2,1)S(1)}, u32[]{:S(2)}, u32[]{:S(2)}) collective-permute-start(bf16[16,4096]{1,0:T(8,128)(2,1)S(1)} %get-tuple-element.1241), channel_id=1, source_target_pairs={{0,8},{8,16},{16,24},{1,9},{9,17},{17,25},{2,10},{10,18},{18,26},{... | collective-permute-start | bytes 393224 | tf_op jit(solution)/shard_map/while/body/eval_jaxpr/ppermute | solution.py:14
  323.3 8.8 %collective-permute-start = (bf16[16,4096]{1,0:T(8,128)(2,1)S(1)}, bf16[16,4096]{1,0:T(8,128)(2,1)S(1)}, u32[]{:S(2)}, u32[]{:S(2)}) collective-permute-start(bf16[16,4096]{1,0:T(8,128)(2,1)S(1)} %get-tuple-element.1241), channel_id=1, source_target_pairs={{0,8},{8,16},{16,24},{1,9},{9,17},{17,25},{2,10},{10,18},{18,26},{... | collective-permute-start | bytes 393224 | tf_op jit(solution)/shard_map/while/body/eval_jaxpr/ppermute | solution.py:14
  337.8 15.7 %collective-permute-start = (bf16[16,4096]{1,0:T(8,128)(2,1)S(1)}, bf16[16,4096]{1,0:T(8,128)(2,1)S(1)}, u32[]{:S(2)}, u32[]{:S(2)}) collective-permute-start(bf16[16,4096]{1,0:T(8,128)(2,1)S(1)} %get-tuple-element.1241), channel_id=1, source_target_pairs={{0,8},{8,16},{16,24},{1,9},{9,17},{17,25},{2,10},{10,18},{18,26},{... | collective-permute-start | bytes 393224 | tf_op jit(solution)/shard_map/while/body/eval_jaxpr/ppermute | solution.py:14
  367.0 11.6 %collective-permute-start.1 = (bf16[16,4096]{1,0:T(8,128)(2,1)S(1)}, bf16[16,4096]{1,0:T(8,128)(2,1)S(1)}, u32[]{:S(2)}, u32[]{:S(2)}) collective-permute-start(bf16[16,4096]{1,0:T(8,128)(2,1)S(1)} %get-tuple-element.1271), channel_id=1, source_target_pairs={{8,0},{16,8},{24,16},{9,1},{17,9},{25,17},{10,2},{18,10},{26,18},{... | collective-permute-start | bytes 393224 | tf_op jit(solution)/shard_map/while/body/eval_jaxpr/ppermute | solution.py:14
  380.4 42.8 %collective-permute-start.1 = (bf16[16,4096]{1,0:T(8,128)(2,1)S(1)}, bf16[16,4096]{1,0:T(8,128)(2,1)S(1)}, u32[]{:S(2)}, u32[]{:S(2)}) collective-permute-start(bf16[16,4096]{1,0:T(8,128)(2,1)S(1)} %get-tuple-element.1271), channel_id=1, source_target_pairs={{8,0},{16,8},{24,16},{9,1},{17,9},{25,17},{10,2},{18,10},{26,18},{... | collective-permute-start | bytes 393224 | tf_op jit(solution)/shard_map/while/body/eval_jaxpr/ppermute | solution.py:14
  437.5 8.1 %collective-permute-start.1 = (bf16[16,4096]{1,0:T(8,128)(2,1)S(1)}, bf16[16,4096]{1,0:T(8,128)(2,1)S(1)}, u32[]{:S(2)}, u32[]{:S(2)}) collective-permute-start(bf16[16,4096]{1,0:T(8,128)(2,1)S(1)} %get-tuple-element.1271), channel_id=1, source_target_pairs={{8,0},{16,8},{24,16},{9,1},{17,9},{25,17},{10,2},{18,10},{26,18},{... | collective-permute-start | bytes 393224 | tf_op jit(solution)/shard_map/while/body/eval_jaxpr/ppermute | solution.py:14
  460.0 8.1 %collective-permute-start.1 = (bf16[16,4096]{1,0:T(8,128)(2,1)S(1)}, bf16[16,4096]{1,0:T(8,128)(2,1)S(1)}, u32[]{:S(2)}, u32[]{:S(2)}) collective-permute-start(bf16[16,4096]{1,0:T(8,128)(2,1)S(1)} %get-tuple-element.1271), channel_id=1, source_target_pairs={{8,0},{16,8},{24,16},{9,1},{17,9},{25,17},{10,2},{18,10},{26,18},{... | collective-permute-start | bytes 393224 | tf_op jit(solution)/shard_map/while/body/eval_jaxpr/ppermute | solution.py:14
  527.4 8.1 %collective-permute-start.1 = (bf16[16,4096]{1,0:T(8,128)(2,1)S(1)}, bf16[16,4096]{1,0:T(8,128)(2,1)S(1)}, u32[]{:S(2)}, u32[]{:S(2)}) collective-permute-start(bf16[16,4096]{1,0:T(8,128)(2,1)S(1)} %get-tuple-element.1271), channel_id=1, source_target_pairs={{8,0},{16,8},{24,16},{9,1},{17,9},{25,17},{10,2},{18,10},{26,18},{... | collective-permute-start | bytes 393224 | tf_op jit(solution)/shard_map/while/body/eval_jaxpr/ppermute | solution.py:14
  549.9 8.1 %collective-permute-start.1 = (bf16[16,4096]{1,0:T(8,128)(2,1)S(1)}, bf16[16,4096]{1,0:T(8,128)(2,1)S(1)}, u32[]{:S(2)}, u32[]{:S(2)}) collective-permute-start(bf16[16,4096]{1,0:T(8,128)(2,1)S(1)} %get-tuple-element.1271), channel_id=1, source_target_pairs={{8,0},{16,8},{24,16},{9,1},{17,9},{25,17},{10,2},{18,10},{26,18},{... | collective-permute-start | bytes 393224 | tf_op jit(solution)/shard_map/while/body/eval_jaxpr/ppermute | solution.py:14
  572.4 8.1 %collective-permute-start.1 = (bf16[16,4096]{1,0:T(8,128)(2,1)S(1)}, bf16[16,4096]{1,0:T(8,128)(2,1)S(1)}, u32[]{:S(2)}, u32[]{:S(2)}) collective-permute-start(bf16[16,4096]{1,0:T(8,128)(2,1)S(1)} %get-tuple-element.1271), channel_id=1, source_target_pairs={{8,0},{16,8},{24,16},{9,1},{17,9},{25,17},{10,2},{18,10},{26,18},{... | collective-permute-start | bytes 393224 | tf_op jit(solution)/shard_map/while/body/eval_jaxpr/ppermute | solution.py:14
  609.0 159.1 %all-gather.19.cloned.1.call-start = ((), (), s32[]{:S(2)}) async-start(), calls=%async_computation.4 | async-start | bytes 9437184 | tf_op jit(solution)/shard_map/all_gather | solution.py:201
  (52 other events, 460.7 us)
Sparse Core Ops, SparseCore 0:
  9.6 25.0 all-gather.10
  36.2 21.8 all-gather.12
  59.7 21.8 all-gather.14
  83.1 21.8 all-gather.16
  609.1 75.4 all-reduce.2
  686.0 82.0 all-gather.18
